TPU v7x, 32 devices: a whole 2x2x4 slice. The times are simulated.
32 devices in a mesh: dp: 4 (over y, core), expert: 2 (over x), tensor: 4 (over z).
Axes of the slice: x: 2, y: 2, z: 4, core: 2. Of those that a mesh axis runs over, the one named last changes fastest.
Arguments:
- inputs: bfloat16 [1576, 768], P(('dp', 'expert')), may hold values from -6 to 6
- first_gain: float32 [768], replicated, may hold values from 0.5 to 1.5
- first_bias: float32 [768], replicated, may hold values from -2 to 2
- attention_in: bfloat16 [3, 768, 768], P(None, None, 'tensor')
- attention_out: bfloat16 [768, 768], P('tensor'), may hold values from -0.875 to 0.875
- second_gain: float32 [768], replicated, may hold values from 0.5 to 1.5
- second_bias: float32 [768], replicated, may hold values from -2 to 2
- router_weight: float32 [768, 4], replicated
- expert_in: bfloat16 [4, 768, 3072], P('expert', None, 'tensor'), may hold values from -0.21875 to 0.21875
- expert_out: bfloat16 [4, 3072, 768], P('expert', 'tensor'), may hold values from -1.75 to 1.75
- expert_ids: int32 [1576, 2], P(('dp', 'expert')), may hold values from 0 to 3, as said below
- slot_index: int32 [1576, 2], P(('dp', 'expert')), may hold values from 0 to 98, as said below
- cotangent: bfloat16 [1576, 768], P(('dp', 'expert')), may hold values from -6 to 6
Outputs:
- layer_out: float32 [1576, 768], P(('dp', 'expert'))
- input_grad: float32 [1576, 768], P(('dp', 'expert'))
- first_gain_grad: float32 [768], P(('dp', 'expert'))
- first_bias_grad: float32 [768], P(('dp', 'expert'))
- attention_in_grad: float32 [3, 768, 768], P(None, ('dp', 'expert'), 'tensor')
- attention_out_grad: float32 [768, 768], P('tensor', ('dp', 'expert'))
- second_gain_grad: float32 [768], P(('dp', 'expert'))
- second_bias_grad: float32 [768], P(('dp', 'expert'))
- router_grad: float32 [768, 4], P(('dp', 'expert'))
- expert_in_grad: float32 [4, 768, 3072], P('expert', 'dp', 'tensor')
- expert_out_grad: float32 [4, 3072, 768], P('expert', 'tensor', 'dp')
Inputs may be any that keep to these rules, and one draw needn't show every extreme that they name: `expert_ids`: the two experts of a token differ. `slot_index`: among the 197 tokens of one index of dp and expert, the choices naming one expert hold slots 0, 1, 2 and so on, all first choices before all second choices, rows in order within each; a choice ranked 98 or later holds 98 and is dropped. Some expert fills all 98 slots from every index of dp and expert.
All inputs are finite; a program needn't handle non-finite values.
Results may differ from a plain program's by a relative error of at most 0.02.
Values may be sent and summed in bfloat16 or wider, within the bound.
A program may use at most 128 MiB of HBM per device.

v0:
```python
import math
import jax
import jax.numpy as jnp
from jax import lax
from jax.sharding import PartitionSpec as P

HEAD_DIM = 64
SEQ = 197
EPS = 1e-06
GELU_C = math.sqrt(2.0 / math.pi)


def cut_along(shard, dim, devices):
    shape = shard.shape
    tiles = shard.reshape(*shape[:dim], devices, shape[dim] // devices, *shape[dim + 1 :])
    return jnp.moveaxis(tiles, dim, 0)


def sent_and_summed(shard, axis, dim):
    devices = lax.axis_size(axis)
    tiles = lax.all_to_all(cut_along(shard, dim, devices), axis, 0, 0, tiled=True)
    return jnp.sum(tiles.astype(jnp.float32), axis=0)


def sent_together(arrays, axis, dim, along):
    widths = [math.prod(a.shape[along:]) for a in arrays]
    both = jnp.concatenate(
        [a.reshape(*a.shape[:along], w) for a, w in zip(arrays, widths)], axis=along
    )
    out = sent_and_summed(both, axis, dim)
    tiles = jnp.split(out, [sum(widths[:k]) for k in range(1, len(widths))], axis=along)
    return tuple((b.reshape(*out.shape[:along], *a.shape[along:]) for a, b in zip(arrays, tiles)))


def normalize(values):
    centre = jnp.mean(values, axis=-1, keepdims=True)
    centred = values - centre
    spread = jnp.mean(centred * centred, axis=-1, keepdims=True)
    scale = lax.rsqrt(spread + EPS)
    return (centred * scale, scale)


def norm_back(grad_out, normed, scale, gain):
    scaled = grad_out * gain
    first_mean = jnp.mean(scaled, axis=-1, keepdims=True)
    second_mean = jnp.mean(scaled * normed, axis=-1, keepdims=True)
    return scale * (scaled - first_mean - normed * second_mean)


def gelu_parts(pre):
    inner = GELU_C * (pre + 0.044715 * pre * pre * pre)
    tangent = jnp.tanh(inner)
    value = 0.5 * pre * (1.0 + tangent)
    slope = 0.5 * (1.0 + tangent) + 0.5 * pre * (1.0 - tangent * tangent) * GELU_C * (
        1.0 + 3.0 * 0.044715 * pre * pre
    )
    return (value, slope)


def per_device(
    inputs,
    first_gain,
    first_bias,
    attention_in,
    attention_out,
    second_gain,
    second_bias,
    router_weight,
    expert_in,
    expert_out,
    expert_ids,
    slot_index,
    cotangent,
):
    tokens_here = inputs.shape[0]
    model_width = inputs.shape[1]
    images = tokens_here // SEQ
    local_width = attention_in.shape[2]
    local_heads = local_width // HEAD_DIM
    owners = lax.axis_size("expert")
    experts_here = expert_in.shape[0]
    experts_all = experts_here * owners
    capacity = (2 * tokens_here - 1) // experts_all
    scaling = HEAD_DIM ** (-0.5)

    def split_heads(matrix):
        return matrix.reshape(images, SEQ, local_heads, HEAD_DIM)

    x_full = inputs.astype(jnp.float32)
    normed1, scale1 = normalize(x_full)
    first = (normed1 * first_gain + first_bias).astype(jnp.bfloat16)
    project = [
        jnp.dot(first, attention_in[which], preferred_element_type=jnp.float32).astype(jnp.bfloat16)
        for which in range(3)
    ]
    query_h, keys_h, values_h = [split_heads(part) for part in project]
    scores = (
        jnp.einsum("iqhd,ikhd->ihqk", query_h, keys_h, preferred_element_type=jnp.float32) * scaling
    )
    peak = jnp.max(scores, axis=-1, keepdims=True)
    logsum = peak[..., 0] + jnp.log(jnp.sum(jnp.exp(scores - peak), axis=-1))
    weights = jnp.exp(scores - logsum[..., None]).astype(jnp.bfloat16)
    context_h = jnp.einsum(
        "ihqk,ikhd->iqhd", weights, values_h, preferred_element_type=jnp.float32
    ).astype(jnp.bfloat16)
    context = context_h.reshape(tokens_here, local_width)
    partial_attn = jnp.dot(context, attention_out, preferred_element_type=jnp.float32)
    attended = lax.psum(partial_attn, "tensor")
    resid = x_full + attended
    normed2, scale2 = normalize(resid)
    second = (normed2 * second_gain + second_bias).astype(jnp.bfloat16)
    logits = jnp.dot(second.astype(jnp.float32), router_weight, precision=lax.Precision.HIGHEST)
    route = jax.nn.softmax(logits, axis=-1)
    valid = (slot_index < capacity).astype(jnp.float32)
    choose = (expert_ids[:, :, None] == jnp.arange(experts_all, dtype=jnp.int32)).astype(
        jnp.float32
    )
    gate = jnp.sum(route[:, None, :] * choose, axis=-1) * valid
    target = jnp.where(slot_index < capacity, expert_ids * capacity + slot_index, -1)
    chosen = (target[:, :, None] == jnp.arange(experts_all * capacity, dtype=jnp.int32)).astype(
        jnp.bfloat16
    )
    placing = jnp.sum(chosen, axis=1)
    sendbuf = jnp.einsum("rq,rd->qd", placing, second, preferred_element_type=jnp.float32).astype(
        jnp.bfloat16
    )
    sendbuf = sendbuf.reshape(owners, experts_here, capacity, model_width)
    received = lax.all_to_all(sendbuf, "expert", split_axis=0, concat_axis=0, tiled=True)
    pre = jnp.einsum("skcd,kdf->skcf", received, expert_in, preferred_element_type=jnp.float32)
    value, slope = gelu_parts(pre)
    hidden = value.astype(jnp.bfloat16)
    partial_value = jnp.einsum(
        "skcf,kfd->skcd", hidden, expert_out, preferred_element_type=jnp.float32
    )
    summed = lax.psum(partial_value, "tensor")
    returned = lax.all_to_all(
        summed.astype(jnp.bfloat16), "expert", split_axis=0, concat_axis=0, tiled=True
    )
    outcome = (returned, received, hidden, slope)
    returned = outcome[0]
    received = outcome[1]
    outputs_flat = returned.reshape(experts_all * capacity, model_width)
    picked = jnp.einsum("rjq,qd->rjd", chosen, outputs_flat, preferred_element_type=jnp.float32)
    layer_out = resid + jnp.sum(gate[..., None] * picked, axis=1)
    grad_out = cotangent.astype(jnp.float32)
    gate_grad = jnp.sum(grad_out[:, None, :] * picked, axis=-1) * valid
    slot_gate = jnp.einsum(
        "rjq,rj->q", chosen.astype(jnp.float32), gate, precision=lax.Precision.HIGHEST
    )
    slotted = jnp.einsum("rq,rd->qd", placing, cotangent, preferred_element_type=jnp.float32)
    grad_send = (
        (slot_gate[:, None] * slotted)
        .astype(jnp.bfloat16)
        .reshape(owners, experts_here, capacity, model_width)
    )
    grad_recv = lax.all_to_all(grad_send, "expert", split_axis=0, concat_axis=0, tiled=True)
    hidden = outcome[2]
    slope = outcome[3]
    hidden_grad = jnp.einsum(
        "skcd,kfd->skcf", grad_recv, expert_out, preferred_element_type=jnp.float32
    )
    pre_grad = (hidden_grad * slope).astype(jnp.bfloat16)
    local_out_grad = jnp.einsum(
        "skcf,skcd->kfd", hidden, grad_recv, preferred_element_type=jnp.float32
    )
    local_in_grad = jnp.einsum(
        "skcd,skcf->kdf", received, pre_grad, preferred_element_type=jnp.float32
    )
    partial_back = jnp.einsum(
        "skcf,kdf->skcd", pre_grad, expert_in, preferred_element_type=jnp.float32
    )
    back_sum = lax.psum(partial_back.astype(jnp.bfloat16), "tensor")
    back_home = lax.all_to_all(back_sum, "expert", split_axis=0, concat_axis=0, tiled=True)
    back_rows = jnp.einsum(
        "rjq,qd->rd",
        chosen,
        back_home.reshape(experts_all * capacity, model_width),
        preferred_element_type=jnp.float32,
    )
    expert_in_grad, expert_out_grad = (
        lax.psum_scatter(
            local_in_grad.astype(jnp.bfloat16), "dp", scatter_dimension=1, tiled=True
        ).astype(jnp.float32),
        lax.psum_scatter(
            local_out_grad.astype(jnp.bfloat16), "dp", scatter_dimension=2, tiled=True
        ).astype(jnp.float32),
    )
    route_grad = jnp.sum(gate_grad[:, :, None] * choose, axis=1)
    logit_grad = route * (route_grad - jnp.sum(route * route_grad, axis=-1, keepdims=True))
    local_router = jnp.dot(
        second.astype(jnp.float32).T, logit_grad, precision=lax.Precision.HIGHEST
    )
    second_grad = back_rows + jnp.dot(logit_grad, router_weight.T, precision=lax.Precision.HIGHEST)
    local_second_gain = jnp.sum(second_grad * normed2, axis=0)
    local_second_bias = jnp.sum(second_grad, axis=0)
    resid_grad = grad_out + norm_back(second_grad, normed2, scale2, second_gain)
    resid_low = resid_grad.astype(jnp.bfloat16)
    local_attn_out = jnp.einsum("rh,rd->hd", context, resid_low, preferred_element_type=jnp.float32)
    context_grad = jnp.einsum(
        "rd,hd->rh", resid_low, attention_out, preferred_element_type=jnp.float32
    ).astype(jnp.bfloat16)
    context_g = split_heads(context_grad)
    probs = jnp.exp(scores - logsum[..., None])
    values_grad = jnp.einsum(
        "ihqk,iqhd->ikhd", weights, context_g, preferred_element_type=jnp.float32
    ).astype(jnp.bfloat16)
    probs_grad = jnp.einsum(
        "iqhd,ikhd->ihqk", context_g, values_h, preferred_element_type=jnp.float32
    )
    delta = jnp.transpose(
        jnp.sum(context_g.astype(jnp.float32) * context_h.astype(jnp.float32), axis=-1), (0, 2, 1)
    )
    score_grad = (probs * (probs_grad - delta[..., None]) * scaling).astype(jnp.bfloat16)
    query_grad = jnp.einsum(
        "ihqk,ikhd->iqhd", score_grad, keys_h, preferred_element_type=jnp.float32
    ).astype(jnp.bfloat16)
    keys_grad = jnp.einsum(
        "ihqk,iqhd->ikhd", score_grad, query_h, preferred_element_type=jnp.float32
    ).astype(jnp.bfloat16)
    grads_flat = [
        part.reshape(tokens_here, local_width) for part in (query_grad, keys_grad, values_grad)
    ]
    local_attn_in = jnp.stack(
        [
            jnp.einsum("rd,rh->dh", first, part, preferred_element_type=jnp.float32)
            for part in grads_flat
        ]
    )
    partial_first = jnp.einsum(
        "rh,dh->rd", grads_flat[0], attention_in[0], preferred_element_type=jnp.float32
    )
    partial_first = partial_first + jnp.einsum(
        "rh,dh->rd", grads_flat[1], attention_in[1], preferred_element_type=jnp.float32
    )
    partial_first = partial_first + jnp.einsum(
        "rh,dh->rd", grads_flat[2], attention_in[2], preferred_element_type=jnp.float32
    )
    first_grad = lax.psum(partial_first.astype(jnp.bfloat16), "tensor").astype(jnp.float32)
    local_first_gain = jnp.sum(first_grad * normed1, axis=0)
    local_first_bias = jnp.sum(first_grad, axis=0)
    input_grad = resid_grad + norm_back(first_grad, normed1, scale1, first_gain)
    summed_shared = (
        sent_and_summed(local_attn_in.astype(jnp.bfloat16), ("dp", "expert"), 1),
        sent_and_summed(local_attn_out.astype(jnp.bfloat16), ("dp", "expert"), 1),
        *sent_together(
            (
                local_router.astype(jnp.bfloat16),
                local_first_gain.astype(jnp.bfloat16),
                local_first_bias.astype(jnp.bfloat16),
                local_second_gain.astype(jnp.bfloat16),
                local_second_bias.astype(jnp.bfloat16),
            ),
            ("dp", "expert"),
            0,
            1,
        ),
    )
    (
        attention_in_grad,
        attention_out_grad,
        router_grad,
        first_gain_grad,
        first_bias_grad,
        second_gain_grad,
        second_bias_grad,
    ) = summed_shared
    return (
        layer_out,
        input_grad,
        first_gain_grad,
        first_bias_grad,
        attention_in_grad,
        attention_out_grad,
        second_gain_grad,
        second_bias_grad,
        router_grad,
        expert_in_grad,
        expert_out_grad,
    )


def solution(mesh):
    in_specs = (
        P(("dp", "expert"), None),
        P(),
        P(),
        P(None, None, "tensor"),
        P("tensor", None),
        P(),
        P(),
        P(),
        P("expert", None, "tensor"),
        P("expert", "tensor", None),
        P(("dp", "expert"), None),
        P(("dp", "expert"), None),
        P(("dp", "expert"), None),
    )
    out_specs = (
        P(("dp", "expert"), None),
        P(("dp", "expert"), None),
        P(("dp", "expert")),
        P(("dp", "expert")),
        P(None, ("dp", "expert"), "tensor"),
        P("tensor", ("dp", "expert")),
        P(("dp", "expert")),
        P(("dp", "expert")),
        P(("dp", "expert"), None),
        P("expert", "dp", "tensor"),
        P("expert", "tensor", "dp"),
    )
    return jax.shard_map(
        per_device, mesh=mesh, in_specs=in_specs, out_specs=out_specs, check_vma=False
    )
```

profile of v0, /device:TPU:0, one launch (start us, length us, event | category | flops | bytes accessed | tf_op | source)
XLA Modules:
  0.0 338.7 jit_solution(17743377087618630051)
XLA Ops:
  15.5 42.5 %all-reduce.5.cloned.1.call-done = f32[197,768]{1,0:T(8,128)} async-done(((f32[197,768]{1,0:T(8,128)}), f32[197,768]{1,0:T(8,128)}) %all-reduce.5.cloned.1.call-update) | async-done | bytes 605200 | tf_op jit(solution)/shard_map/psum | solution.py:108
  63.6 2.4 copy.130
  66.0 4.2 %all-to-all-start = ((bf16[2,2,98,768]{3,1,2,0:T(2,128)(2,1)}), bf16[2,2,98,768]{3,1,2,0:T(2,128)(2,1)}, u32[]{:S(2)}, u32[]{:S(2)}) async-start(bf16[2,2,98,768]{3,1,2,0:T(2,128)(2,1)} %copy.130), calls=%async_computation | async-start | bytes 1204224 | tf_op jit(solution)/shard_map/all_to_all | solution.py:128
  74.9 2.4 copy.134
  78.8 4.3 %all-to-all-start.2 = ((bf16[2,2,98,768]{3,1,2,0:T(2,128)(2,1)}), bf16[2,2,98,768]{3,1,2,0:T(2,128)(2,1)}, u32[]{:S(2)}, u32[]{:S(2)}) async-start(bf16[2,2,98,768]{3,1,2,0:T(2,128)(2,1)} %copy.134), calls=%async_computation.2 | async-start | bytes 1204224 | tf_op jit(solution)/shard_map/all_to_all | solution.py:156
  83.1 2.5 fusion.14
  89.5 47.3 %all-reduce.10 = bf16[2,2,98,768]{3,1,2,0:T(2,128)(2,1)} all-reduce(f32[2,2,98,768]{3,1,2,0:T(2,128)} %bitcast.163), channel_id=1, replica_groups=mesh['dp'=4,'expert'=2,'tensor'=4] {'tensor'}, use_global_device_ids=true, to_apply=%region_11.12 | all-reduce | flops 301056 | bytes 1806336 | tf_op jit(solution)/shard_map/psum | solution.py:135
  136.7 4.3 %all-to-all-start.1 = ((bf16[2,2,98,768]{3,1,2,0:T(2,128)(2,1)}), bf16[2,2,98,768]{3,1,2,0:T(2,128)(2,1)}, u32[]{:S(2)}, u32[]{:S(2)}) async-start(bf16[2,2,98,768]{3,1,2,0:T(2,128)(2,1)} %all-reduce.10), calls=%async_computation.1 | async-start | bytes 1204224 | tf_op jit(solution)/shard_map/all_to_all | solution.py:136
  141.1 2.9 fusion.17
  152.4 2.8 multiply_reduce_fusion
  155.3 31.0 %all-reduce.7.cloned.1.call-done = bf16[2,2,98,768]{3,2,0,1:T(8,128)(2,1)} async-done(((bf16[2,2,98,768]{3,2,0,1:T(8,128)(2,1)}), bf16[2,2,98,768]{3,2,0,1:T(8,128)(2,1)}) %all-reduce.7.cloned.1.call-update) | async-done | bytes 602128 | tf_op jit(solution)/shard_map/psum | solution.py:172
  186.3 2.4 copy.136
  188.6 4.2 %all-to-all-start.3 = ((bf16[2,2,98,768]{3,1,2,0:T(2,128)(2,1)}), bf16[2,2,98,768]{3,1,2,0:T(2,128)(2,1)}, u32[]{:S(2)}, u32[]{:S(2)}) async-start(bf16[2,2,98,768]{3,1,2,0:T(2,128)(2,1)} %copy.136), calls=%async_computation.3 | async-start | bytes 1204224 | tf_op jit(solution)/shard_map/all_to_all | solution.py:173
  194.7 6.8 %all-to-all-done.3 = bf16[2,2,98,768]{3,1,2,0:T(2,128)(2,1)} async-done(((bf16[2,2,98,768]{3,1,2,0:T(2,128)(2,1)}), bf16[2,2,98,768]{3,1,2,0:T(2,128)(2,1)}, u32[]{:S(2)}, u32[]{:S(2)}) %all-to-all-start.3) | async-done | bytes 602144 | tf_op jit(solution)/shard_map/all_to_all | solution.py:173
  212.7 3.3 bitcast_convert_fusion.1
  216.1 3.8 %bitcast_convert_fusion = bf16[2,768,768]{1,2,0:T(8,128)(2,1)} fusion(bf16[2,2,98,768]{3,1,2,0:T(2,128)(2,1)} %all-to-all-done.2, f32[2,2,98,768]{3,2,0,1:T(8,128)} %copy-done.14), kind=kOutput, calls=%fused_computation | convolution fusion | flops 466311168 | bytes 4165632 | tf_op jit(solution)/shard_map/skcf,skcd->kfd/dot_general | solution.py:163
  226.0 4.1 %all-to-all-start.6 = ((bf16[8,192,96]{2,1,0:T(8,128)(2,1)}), bf16[8,192,96]{2,1,0:T(8,128)(2,1)}, u32[]{:S(2)}, u32[]{:S(2)}) async-start(bf16[8,192,96]{2,1,0:T(8,128)(2,1)} %bitcast.164), calls=%async_computation.6 | async-start | bytes 786432 | tf_op jit(solution)/shard_map/all_to_all | solution.py:21
  231.6 6.3 %all-to-all-done.6 = bf16[8,192,96]{2,1,0:T(8,128)(2,1)} async-done(((bf16[8,192,96]{2,1,0:T(8,128)(2,1)}), bf16[8,192,96]{2,1,0:T(8,128)(2,1)}, u32[]{:S(2)}, u32[]{:S(2)}) %all-to-all-start.6) | async-done | bytes 294944 | tf_op jit(solution)/shard_map/all_to_all | solution.py:21
  239.5 8.2 %all-reduce.9.cloned.1.call-done = bf16[197,768]{1,0:T(8,128)(2,1)} async-done(((bf16[197,768]{1,0:T(8,128)(2,1)}), bf16[197,768]{1,0:T(8,128)(2,1)}) %all-reduce.9.cloned.1.call-update) | async-done | bytes 302608 | tf_op jit(solution)/shard_map/psum | solution.py:238
  251.6 3.6 %all-to-all-start.4 = ((bf16[8,96,8]{1,2,0:T(8,128)(2,1)}), bf16[8,96,8]{1,2,0:T(8,128)(2,1)S(1)}, u32[]{:S(2)}, u32[]{:S(2)}) async-start(bf16[8,96,8]{1,2,0:T(8,128)(2,1)} %concatenate.12), calls=%async_computation.4 | async-start | bytes 32768 | tf_op jit(solution)/shard_map/all_to_all | solution.py:21
  261.5 4.3 %all-to-all-start.5 = ((bf16[8,3,96,192]{3,2,1,0:T(8,128)(2,1)}), bf16[8,3,96,192]{3,2,1,0:T(8,128)(2,1)}, u32[]{:S(2)}, u32[]{:S(2)}) async-start(bf16[8,3,96,192]{3,2,1,0:T(8,128)(2,1)} %copy.150), calls=%async_computation.5 | async-start | bytes 2359296 | tf_op jit(solution)/shard_map/all_to_all | solution.py:21
  269.0 19.1 %all-to-all-done.5 = bf16[8,3,96,192]{3,2,1,0:T(8,128)(2,1)} async-done(((bf16[8,3,96,192]{3,2,1,0:T(8,128)(2,1)}), bf16[8,3,96,192]{3,2,1,0:T(8,128)(2,1)}, u32[]{:S(2)}, u32[]{:S(2)}) %all-to-all-start.5) | async-done | bytes 884768 | tf_op jit(solution)/shard_map/all_to_all | solution.py:21
  290.2 5.2 %reduce-scatter.3.cloned.1.call-done = bf16[2,192,768]{2,1,0:T(8,128)(2,1)} async-done(((bf16[2,768,768]{2,1,0:T(8,128)(2,1)}), bf16[2,192,768]{2,1,0:T(8,128)(2,1)}) %reduce-scatter.3.cloned.1.call-update) | async-done | bytes 589840 | tf_op jit(solution)/shard_map/reduce_scatter | solution.py:181
  297.6 32.4 %reduce-scatter.5.cloned.1.call-done = bf16[2,768,192]{1,2,0:T(8,128)(2,1)} async-done(((bf16[2,768,768]{1,2,0:T(8,128)(2,1)}), bf16[2,768,192]{1,2,0:T(8,128)(2,1)}) %reduce-scatter.5.cloned.1.call-update) | async-done | bytes 589840 | tf_op jit(solution)/shard_map/reduce_scatter | solution.py:184
  (178 shorter events, 74.1 us)
Async XLA Ops:
  7.2 79.5 %copy-start = (bf16[2,768,768]{2,1,0:T(8,128)(2,1)S(1)}, bf16[2,768,768]{2,1,0:T(8,128)(2,1)}, u32[]{:S(2)}) copy-start(bf16[2,768,768]{2,1,0:T(8,128)(2,1)} %param.22) | copy-start | bytes 7077892
  7.2 4.1 %copy-start.6 = (bf16[197,768]{1,0:T(8,128)(2,1)S(1)}, bf16[197,768]{1,0:T(8,128)(2,1)}, u32[]{:S(2)}) copy-start(bf16[197,768]{1,0:T(8,128)(2,1)} %param.13) | copy-start | bytes 907780
  7.2 4.1 %copy-start.17 = (bf16[3,768,192]{1,2,0:T(8,128)(2,1)S(1)}, bf16[3,768,192]{1,2,0:T(8,128)(2,1)}, u32[]{:S(2)}) copy-start(bf16[3,768,192]{1,2,0:T(8,128)(2,1)} %param.16) | copy-start | bytes 2654212
  7.2 50.8 %all-reduce.5.cloned.1.call-start = ((), (), s32[]{:S(2)}) async-start(), calls=%async_computation.9 | async-start | bytes 1228800 | tf_op jit(solution)/shard_map/psum | solution.py:108
  7.3 4.0 %copy-start.34 = (f32[768]{0:T(1024)S(1)}, f32[768]{0:T(1024)}, u32[]{:S(2)}) copy-start(f32[768]{0:T(1024)} %param.14) | copy-start | bytes 9220
  7.3 4.0 %copy-start.39 = (f32[768]{0:T(1024)S(1)}, f32[768]{0:T(1024)}, u32[]{:S(2)}) copy-start(f32[768]{0:T(1024)} %param.15) | copy-start | bytes 9220
  15.3 44.1 %copy-start.31 = (f32[768]{0:T(1024)S(1)}, f32[768]{0:T(1024)}, u32[]{:S(2)}) copy-start(f32[768]{0:T(1024)} %param.18) | copy-start | bytes 9220
  15.3 44.1 %copy-start.38 = (f32[768]{0:T(1024)S(1)}, f32[768]{0:T(1024)}, u32[]{:S(2)}) copy-start(f32[768]{0:T(1024)} %param.19) | copy-start | bytes 9220
  15.5 44.2 %copy-start.30 = (f32[768,4]{0,1:T(4,128)S(1)}, f32[768,4]{0,1:T(4,128)}, u32[]{:S(2)}) copy-start(f32[768,4]{0,1:T(4,128)} %param.20) | copy-start | bytes 36868
  66.0 12.8 %all-to-all-start = ((bf16[2,2,98,768]{3,1,2,0:T(2,128)(2,1)}), bf16[2,2,98,768]{3,1,2,0:T(2,128)(2,1)}, u32[]{:S(2)}, u32[]{:S(2)}) async-start(bf16[2,2,98,768]{3,1,2,0:T(2,128)(2,1)} %copy.130), calls=%async_computation | async-start | bytes 1204224 | tf_op jit(solution)/shard_map/all_to_all | solution.py:128
  78.8 58.0 %all-to-all-start.2 = ((bf16[2,2,98,768]{3,1,2,0:T(2,128)(2,1)}), bf16[2,2,98,768]{3,1,2,0:T(2,128)(2,1)}, u32[]{:S(2)}, u32[]{:S(2)}) async-start(bf16[2,2,98,768]{3,1,2,0:T(2,128)(2,1)} %copy.134), calls=%async_computation.2 | async-start | bytes 1204224 | tf_op jit(solution)/shard_map/all_to_all | solution.py:156
  136.7 11.6 %all-to-all-start.1 = ((bf16[2,2,98,768]{3,1,2,0:T(2,128)(2,1)}), bf16[2,2,98,768]{3,1,2,0:T(2,128)(2,1)}, u32[]{:S(2)}, u32[]{:S(2)}) async-start(bf16[2,2,98,768]{3,1,2,0:T(2,128)(2,1)} %all-reduce.10), calls=%async_computation.1 | async-start | bytes 1204224 | tf_op jit(solution)/shard_map/all_to_all | solution.py:136
  141.0 45.3 %all-reduce.7.cloned.1.call-start = ((), (), s32[]{:S(2)}) async-start(), calls=%async_computation.10 | async-start | bytes 1277952 | tf_op jit(solution)/shard_map/psum | solution.py:172
  188.6 12.9 %all-to-all-start.3 = ((bf16[2,2,98,768]{3,1,2,0:T(2,128)(2,1)}), bf16[2,2,98,768]{3,1,2,0:T(2,128)(2,1)}, u32[]{:S(2)}, u32[]{:S(2)}) async-start(bf16[2,2,98,768]{3,1,2,0:T(2,128)(2,1)} %copy.136), calls=%async_computation.3 | async-start | bytes 1204224 | tf_op jit(solution)/shard_map/all_to_all | solution.py:173
  192.9 54.9 %all-reduce.9.cloned.1.call-start = ((), (), s32[]{:S(2)}) async-start(), calls=%async_computation.11 | async-start | bytes 614400 | tf_op jit(solution)/shard_map/psum | solution.py:238
  212.7 82.8 %reduce-scatter.3.cloned.1.call-start = ((), (), s32[]{:S(2)}) async-start(), calls=%async_computation.12 | async-start | bytes 2949120 | tf_op jit(solution)/shard_map/reduce_scatter | solution.py:181
  216.1 113.9 %reduce-scatter.5.cloned.1.call-start = ((), (), s32[]{:S(2)}) async-start(), calls=%async_computation.13 | async-start | bytes 2949120 | tf_op jit(solution)/shard_map/reduce_scatter | solution.py:184
  224.1 23.6 %copy-start.35 = (f32[768]{0:T(1024)S(1)}, f32[768]{0:T(1024)}, u32[]{:S(2)}) copy-start(f32[768]{0:T(1024)} %param.14) | copy-start | bytes 9220
  224.1 23.6 %copy-start.37 = (f32[197]{0:T(256)S(1)}, f32[197]{0:T(256)}, u32[]{:S(2)}) copy-start(f32[197]{0:T(256)} %copy-done.36) | copy-start | bytes 2368
  224.1 23.6 %copy-start.40 = (f32[768]{0:T(1024)S(1)}, f32[768]{0:T(1024)}, u32[]{:S(2)}) copy-start(f32[768]{0:T(1024)} %param.15) | copy-start | bytes 9220
  226.0 11.9 %all-to-all-start.6 = ((bf16[8,192,96]{2,1,0:T(8,128)(2,1)}), bf16[8,192,96]{2,1,0:T(8,128)(2,1)}, u32[]{:S(2)}, u32[]{:S(2)}) async-start(bf16[8,192,96]{2,1,0:T(8,128)(2,1)} %bitcast.164), calls=%async_computation.6 | async-start | bytes 786432 | tf_op jit(solution)/shard_map/all_to_all | solution.py:21
  239.5 18.9 %copy-start.20 = (bf16[3,64,197]{2,1,0:T(8,128)(2,1)S(1)}, bf16[3,64,197]{2,1,0:T(8,128)(2,1)}, u32[]{:S(2)}) copy-start(bf16[3,64,197]{2,1,0:T(8,128)(2,1)} %copy-done.19) | copy-start | bytes 226948
  251.6 9.9 %all-to-all-start.4 = ((bf16[8,96,8]{1,2,0:T(8,128)(2,1)}), bf16[8,96,8]{1,2,0:T(8,128)(2,1)S(1)}, u32[]{:S(2)}, u32[]{:S(2)}) async-start(bf16[8,96,8]{1,2,0:T(8,128)(2,1)} %concatenate.12), calls=%async_computation.4 | async-start | bytes 32768 | tf_op jit(solution)/shard_map/all_to_all | solution.py:21
  261.5 26.5 %all-to-all-start.5 = ((bf16[8,3,96,192]{3,2,1,0:T(8,128)(2,1)}), bf16[8,3,96,192]{3,2,1,0:T(8,128)(2,1)}, u32[]{:S(2)}, u32[]{:S(2)}) async-start(bf16[8,3,96,192]{3,2,1,0:T(8,128)(2,1)} %copy.150), calls=%async_computation.5 | async-start | bytes 2359296 | tf_op jit(solution)/shard_map/all_to_all | solution.py:21
  (29 other events, 46.4 us)
Sparse Core Ops, SparseCore 0:
  15.4 42.5 all-reduce.4
  146.6 39.5 all-reduce.6
  212.8 34.9 all-reduce.8
  250.1 45.2 reduce-scatter.2
  297.8 32.1 reduce-scatter.4
where the time goes:
time: 341 us; the launch traced here: 339 us
  waiting for transfers between devices  153 us (45%)
  blocking collectives  47.3 us (14%)
  matrix products  37.3 us (11%)
  local copies, waits for them, and re-layouts  36.2 us (11%)
  starting transfers between devices  29.3 us (9%)
  other arithmetic  21 us (6%)
  between operations  14.5 us (4%)
    psum x1, blocking collectives, per_device(): summed = lax.psum(partial_value, 'tensor')  47.3 us
    psum x1, waiting for transfers between devices, per_device(): attended = lax.psum(partial_attn, 'tensor')  42.5 us
    reduce_scatter x1, waiting for transfers between devices, per_device(): lax.psum_scatter(local_out_grad.astype(jnp.bfloat16), 'dp', scatter_dimen...  32.4 us
    psum x1, waiting for transfers between devices, per_device(): back_sum = lax.psum(partial_back.astype(jnp.bfloat16), 'tensor')  31 us
    all_to_all x3, waiting for transfers between devices, sent_and_summed(): lax.all_to_all(cut_along(shard, dim, devices), axis, 0, 0, tiled=True)  25.3 us
    all_to_all x3, starting transfers between devices, sent_and_summed(): lax.all_to_all(cut_along(shard, dim, devices), axis, 0, 0, tiled=True)  11.9 us
    psum x1, waiting for transfers between devices, per_device(): lax.psum(partial_first.astype(jnp.bfloat16), 'tensor').astype(jnp.float32)  8.2 us
    all_to_all x1, waiting for transfers between devices, per_device(): lax.all_to_all(back_sum, 'expert', split_axis=0, concat_axis=0, tiled=True)  6.82 us
  transfers between devices with their start and end apart: 12, of which 9 were waited for; matrix products, arithmetic and copies ran while one was open for 18% of the time, Pallas kernels for 0%

commit v1 on v0

--- a/solution.py
+++ b/solution.py
@@ -132,7 +132,9 @@
     partial_value = jnp.einsum(
         "skcf,kfd->skcd", hidden, expert_out, preferred_element_type=jnp.float32
     )
-    summed = lax.psum(partial_value, "tensor")
+    summed = partial_value
+    for hop in (1, 2):
+        summed = summed + lax.ppermute(summed, "tensor", [(dev, dev ^ hop) for dev in range(4)])
     returned = lax.all_to_all(
         summed.astype(jnp.bfloat16), "expert", split_axis=0, concat_axis=0, tiled=True
     )

time: 341 us -> 356 us (1.044)
  waiting for transfers between devices: 153 us -> 204 us
  blocking collectives: 47.3 us -> 10.9 us
  matrix products: 37.3 us -> 31.6 us
  local copies, waits for them, and re-layouts: 36.2 us -> 41.7 us
  other arithmetic: 21 us -> 24.6 us
    psum x1 -> x0, blocking collectives: 47.3 us -> none  [per_device(): summed = lax.psum(partial_value, 'tensor')]
    psum x1, waiting for transfers between devices: 31 us -> 60.9 us  [per_device(): back_sum = lax.psum(partial_back.astype(jnp.bfloat16), 'tensor')]
    ppermute x0 -> x2, waiting for transfers between devices: none -> 15.6 us  [per_device(): lax.ppermute(summed, 'tensor', [(dev, dev ^ hop) for dev in range(4)])]
    all_to_all x0 -> x1, blocking collectives: none -> 10.9 us  [per_device(): lax.all_to_all(sendbuf, 'expert', split_axis=0, concat_axis=0, tiled=True)]
    psum x1, waiting for transfers between devices: 8.2 us -> 13.8 us  [per_device(): lax.psum(partial_first.astype(jnp.bfloat16), 'tensor').astype(jnp.float32)]
    all_to_all x1 -> x0, starting transfers between devices: 4.24 us -> none  [per_device(): lax.all_to_all(sendbuf, 'expert', split_axis=0, concat_axis=0, tiled=True)]
    unnamed x82 -> x92, local copies, waits for them, and re-layouts: 5.77 us -> 8.67 us
  transfers between devices with their start and end apart: 12 -> 13, of which waited for: 9 -> 11; matrix products, arithmetic and copies ran while one was open for 18% -> 17% of each run, Pallas kernels for 0% -> 0%
where the time goes in v1:
time: 356 us; the launch traced here: 354 us
  waiting for transfers between devices  204 us (57%)
  local copies, waits for them, and re-layouts  41.7 us (12%)
  matrix products  31.6 us (9%)
  starting transfers between devices  26.7 us (8%)
  other arithmetic  24.6 us (7%)
  between operations  14.5 us (4%)
  blocking collectives  10.9 us (3%)
    psum x1, waiting for transfers between devices, per_device(): back_sum = lax.psum(partial_back.astype(jnp.bfloat16), 'tensor')  60.9 us
    psum x1, waiting for transfers between devices, per_device(): attended = lax.psum(partial_attn, 'tensor')  42.5 us
    reduce_scatter x1, waiting for transfers between devices, per_device(): lax.psum_scatter(local_out_grad.astype(jnp.bfloat16), 'dp', scatter_dimen...  32.4 us
    all_to_all x3, waiting for transfers between devices, sent_and_summed(): lax.all_to_all(cut_along(shard, dim, devices), axis, 0, 0, tiled=True)  25.7 us
    ppermute x2, waiting for transfers between devices, per_device(): lax.ppermute(summed, 'tensor', [(dev, dev ^ hop) for dev in range(4)])  15.6 us
    psum x1, waiting for transfers between devices, per_device(): lax.psum(partial_first.astype(jnp.bfloat16), 'tensor').astype(jnp.float32)  13.8 us
    all_to_all x3, starting transfers between devices, sent_and_summed(): lax.all_to_all(cut_along(shard, dim, devices), axis, 0, 0, tiled=True)  11.9 us
    all_to_all x1, blocking collectives, per_device(): lax.all_to_all(sendbuf, 'expert', split_axis=0, concat_axis=0, tiled=True)  10.9 us
  transfers between devices with their start and end apart: 13, of which 11 were waited for; matrix products, arithmetic and copies ran while one was open for 17% of the time, Pallas kernels for 0%

profile of v1, /device:TPU:0, one launch (start us, length us, event | category | flops | bytes accessed | tf_op | source)
XLA Modules:
  0.0 354.0 jit_solution(6454791159591241539)
XLA Ops:
  15.5 42.5 %all-reduce.4.cloned.1.call-done = f32[197,768]{1,0:T(8,128)} async-done(((f32[197,768]{1,0:T(8,128)}), f32[197,768]{1,0:T(8,128)}) %all-reduce.4.cloned.1.call-update) | async-done | bytes 605200 | tf_op jit(solution)/shard_map/psum | solution.py:108
  65.2 10.9 %all_to_all.35 = bf16[2,2,98,768]{3,1,2,0:T(2,128)(2,1)S(1)} all-to-all(bf16[2,2,98,768]{3,1,2,0:T(2,128)(2,1)S(1)} %copy.113), channel_id=1, replica_groups=mesh['dp'=4,'expert'=2,'tensor'=4] {'expert'}, dimensions={0} | all-to-all | bytes 1204224 | tf_op jit(solution)/shard_map/all_to_all | solution.py:128
  86.3 2.4 copy.121
  88.7 4.2 %all-to-all-start.2 = ((bf16[2,2,98,768]{3,1,2,0:T(2,128)(2,1)}), bf16[2,2,98,768]{3,1,2,0:T(2,128)(2,1)}, u32[]{:S(2)}, u32[]{:S(2)}) async-start(bf16[2,2,98,768]{3,1,2,0:T(2,128)(2,1)} %copy.121), calls=%async_computation.2 | async-start | bytes 1204224 | tf_op jit(solution)/shard_map/all_to_all | solution.py:158
  92.9 15.6 %collective-permute-done = f32[2,2,98,768]{3,1,2,0:T(2,128)} collective-permute-done((f32[2,2,98,768]{3,1,2,0:T(2,128)}, f32[2,2,98,768]{3,1,2,0:T(2,128)}, u32[]{:S(2)}, u32[]{:S(2)}) %collective-permute-start) | collective-permute-done | bytes 1204256 | tf_op jit(solution)/shard_map/ppermute | solution.py:137
  114.5 2.9 fusion.20
  120.0 60.9 %all-reduce.6.cloned.1.call-done = bf16[2,2,98,768]{3,2,0,1:T(8,128)(2,1)} async-done(((bf16[2,2,98,768]{3,2,0,1:T(8,128)(2,1)}), bf16[2,2,98,768]{3,2,0,1:T(8,128)(2,1)}) %all-reduce.6.cloned.1.call-update) | async-done | bytes 602128 | tf_op jit(solution)/shard_map/psum | solution.py:174
  180.9 2.4 copy.123
  183.2 4.2 %all-to-all-start.3 = ((bf16[2,2,98,768]{3,1,2,0:T(2,128)(2,1)}), bf16[2,2,98,768]{3,1,2,0:T(2,128)(2,1)}, u32[]{:S(2)}, u32[]{:S(2)}) async-start(bf16[2,2,98,768]{3,1,2,0:T(2,128)(2,1)} %copy.123), calls=%async_computation.3 | async-start | bytes 1204224 | tf_op jit(solution)/shard_map/all_to_all | solution.py:175
  190.6 5.8 %all-to-all-done.3 = bf16[2,2,98,768]{3,1,2,0:T(2,128)(2,1)} async-done(((bf16[2,2,98,768]{3,1,2,0:T(2,128)(2,1)}), bf16[2,2,98,768]{3,1,2,0:T(2,128)(2,1)}, u32[]{:S(2)}, u32[]{:S(2)}) %all-to-all-start.3) | async-done | bytes 602144 | tf_op jit(solution)/shard_map/all_to_all | solution.py:175
  196.4 4.4 %all-to-all-start.1 = ((bf16[2,2,98,768]{3,1,2,0:T(2,128)(2,1)}), bf16[2,2,98,768]{3,1,2,0:T(2,128)(2,1)}, u32[]{:S(2)}, u32[]{:S(2)}) async-start(bf16[2,2,98,768]{3,1,2,0:T(2,128)(2,1)} %copy.119), calls=%async_computation.1 | async-start | bytes 1204224 | tf_op jit(solution)/shard_map/all_to_all | solution.py:138
  206.8 2.2 all-to-all-done.1
  222.3 3.3 bitcast_convert_fusion.1
  225.6 3.8 %bitcast_convert_fusion = bf16[2,768,768]{1,2,0:T(8,128)(2,1)} fusion(bf16[2,2,98,768]{3,1,2,0:T(2,128)(2,1)} %all-to-all-done.2, f32[2,2,98,768]{3,2,0,1:T(8,128)} %copy-done.21), kind=kOutput, calls=%fused_computation | convolution fusion | flops 466311168 | bytes 4165632 | tf_op jit(solution)/shard_map/skcf,skcd->kfd/dot_general | solution.py:165
  231.5 2.2 reshape.295
  235.5 4.1 %all-to-all-start.6 = ((bf16[8,192,96]{2,1,0:T(8,128)(2,1)}), bf16[8,192,96]{2,1,0:T(8,128)(2,1)}, u32[]{:S(2)}, u32[]{:S(2)}) async-start(bf16[8,192,96]{2,1,0:T(8,128)(2,1)} %bitcast.164), calls=%async_computation.6 | async-start | bytes 786432 | tf_op jit(solution)/shard_map/all_to_all | solution.py:21
  241.1 6.3 %all-to-all-done.6 = bf16[8,192,96]{2,1,0:T(8,128)(2,1)} async-done(((bf16[8,192,96]{2,1,0:T(8,128)(2,1)}), bf16[8,192,96]{2,1,0:T(8,128)(2,1)}, u32[]{:S(2)}, u32[]{:S(2)}) %all-to-all-start.6) | async-done | bytes 294944 | tf_op jit(solution)/shard_map/all_to_all | solution.py:21
  249.1 13.8 %all-reduce.8.cloned.1.call-done = bf16[197,768]{1,0:T(8,128)(2,1)} async-done(((bf16[197,768]{1,0:T(8,128)(2,1)}), bf16[197,768]{1,0:T(8,128)(2,1)}) %all-reduce.8.cloned.1.call-update) | async-done | bytes 302608 | tf_op jit(solution)/shard_map/psum | solution.py:240
  268.6 3.6 %all-to-all-start.4 = ((bf16[8,96,8]{1,2,0:T(8,128)(2,1)}), bf16[8,96,8]{1,2,0:T(8,128)(2,1)S(1)}, u32[]{:S(2)}, u32[]{:S(2)}) async-start(bf16[8,96,8]{1,2,0:T(8,128)(2,1)} %concatenate.12), calls=%async_computation.4 | async-start | bytes 32768 | tf_op jit(solution)/shard_map/all_to_all | solution.py:21
  276.9 4.3 %all-to-all-start.5 = ((bf16[8,3,96,192]{3,2,1,0:T(8,128)(2,1)}), bf16[8,3,96,192]{3,2,1,0:T(8,128)(2,1)}, u32[]{:S(2)}, u32[]{:S(2)}) async-start(bf16[8,3,96,192]{3,2,1,0:T(8,128)(2,1)} %copy.137), calls=%async_computation.5 | async-start | bytes 2359296 | tf_op jit(solution)/shard_map/all_to_all | solution.py:21
  284.3 19.1 %all-to-all-done.5 = bf16[8,3,96,192]{3,2,1,0:T(8,128)(2,1)} async-done(((bf16[8,3,96,192]{3,2,1,0:T(8,128)(2,1)}), bf16[8,3,96,192]{3,2,1,0:T(8,128)(2,1)}, u32[]{:S(2)}, u32[]{:S(2)}) %all-to-all-start.5) | async-done | bytes 884768 | tf_op jit(solution)/shard_map/all_to_all | solution.py:21
  303.4 2.2 convert_reduce_fusion
  305.6 5.1 %reduce-scatter.3.cloned.1.call-done = bf16[2,192,768]{2,1,0:T(8,128)(2,1)} async-done(((bf16[2,768,768]{2,1,0:T(8,128)(2,1)}), bf16[2,192,768]{2,1,0:T(8,128)(2,1)}) %reduce-scatter.3.cloned.1.call-update) | async-done | bytes 589840 | tf_op jit(solution)/shard_map/reduce_scatter | solution.py:183
  312.9 32.4 %reduce-scatter.5.cloned.1.call-done = bf16[2,768,192]{1,2,0:T(8,128)(2,1)} async-done(((bf16[2,768,768]{1,2,0:T(8,128)(2,1)}), bf16[2,768,192]{1,2,0:T(8,128)(2,1)}) %reduce-scatter.5.cloned.1.call-update) | async-done | bytes 589840 | tf_op jit(solution)/shard_map/reduce_scatter | solution.py:186
  (194 shorter events, 81.1 us)
Async XLA Ops:
  7.2 71.5 %copy-start = (bf16[2,768,768]{2,1,0:T(8,128)(2,1)S(1)}, bf16[2,768,768]{2,1,0:T(8,128)(2,1)}, u32[]{:S(2)}) copy-start(bf16[2,768,768]{2,1,0:T(8,128)(2,1)} %param.22) | copy-start | bytes 7077892
  7.2 4.1 %copy-start.8 = (bf16[197,768]{1,0:T(8,128)(2,1)S(1)}, bf16[197,768]{1,0:T(8,128)(2,1)}, u32[]{:S(2)}) copy-start(bf16[197,768]{1,0:T(8,128)(2,1)} %param.13) | copy-start | bytes 907780
  7.2 4.1 %copy-start.24 = (bf16[3,768,192]{1,2,0:T(8,128)(2,1)S(1)}, bf16[3,768,192]{1,2,0:T(8,128)(2,1)}, u32[]{:S(2)}) copy-start(bf16[3,768,192]{1,2,0:T(8,128)(2,1)} %param.16) | copy-start | bytes 2654212
  7.2 50.8 %all-reduce.4.cloned.1.call-start = ((), (), s32[]{:S(2)}) async-start(), calls=%async_computation.9 | async-start | bytes 1228800 | tf_op jit(solution)/shard_map/psum | solution.py:108
  7.3 4.0 %copy-start.39 = (f32[768]{0:T(1024)S(1)}, f32[768]{0:T(1024)}, u32[]{:S(2)}) copy-start(f32[768]{0:T(1024)} %param.14) | copy-start | bytes 9220
  15.3 44.1 %copy-start.36 = (f32[768]{0:T(1024)S(1)}, f32[768]{0:T(1024)}, u32[]{:S(2)}) copy-start(f32[768]{0:T(1024)} %param.18) | copy-start | bytes 9220
  15.3 44.1 %copy-start.43 = (f32[768]{0:T(1024)S(1)}, f32[768]{0:T(1024)}, u32[]{:S(2)}) copy-start(f32[768]{0:T(1024)} %param.19) | copy-start | bytes 9220
  63.5 13.4 %copy-start.6 = (bf16[2,768,768]{2,1,0:T(8,128)(2,1)S(1)}, bf16[2,768,768]{2,1,0:T(8,128)(2,1)}, u32[]{:S(2)}) copy-start(bf16[2,768,768]{2,1,0:T(8,128)(2,1)} %param.21) | copy-start | bytes 7077892
  81.6 26.9 %collective-permute-start = (f32[2,2,98,768]{3,1,2,0:T(2,128)}, f32[2,2,98,768]{3,1,2,0:T(2,128)}, u32[]{:S(2)}, u32[]{:S(2)}) collective-permute-start(f32[2,2,98,768]{3,1,2,0:T(2,128)} %copy.115), channel_id=1, source_target_pairs={{0,1},{1,0},{2,3},{3,2},{4,5},{5,4},{6,7},{7,6},{8,9},{9,8},{10,11... | collective-permute-start | bytes 3612680 | tf_op jit(solution)/shard_map/ppermute | solution.py:137
  88.7 25.9 %all-to-all-start.2 = ((bf16[2,2,98,768]{3,1,2,0:T(2,128)(2,1)}), bf16[2,2,98,768]{3,1,2,0:T(2,128)(2,1)}, u32[]{:S(2)}, u32[]{:S(2)}) async-start(bf16[2,2,98,768]{3,1,2,0:T(2,128)(2,1)} %copy.121), calls=%async_computation.2 | async-start | bytes 1204224 | tf_op jit(solution)/shard_map/all_to_all | solution.py:158
  92.9 88.0 %all-reduce.6.cloned.1.call-start = ((), (), s32[]{:S(2)}) async-start(), calls=%async_computation.10 | async-start | bytes 1277952 | tf_op jit(solution)/shard_map/psum | solution.py:174
  113.4 74.1 %collective-permute-start.1 = (f32[2,2,98,768]{3,1,2,0:T(2,128)}, f32[2,2,98,768]{3,1,2,0:T(2,128)}, u32[]{:S(2)}, u32[]{:S(2)}) collective-permute-start(f32[2,2,98,768]{3,1,2,0:T(2,128)} %copy.117), channel_id=1, source_target_pairs={{0,2},{1,3},{2,0},{3,1},{4,6},{5,7},{6,4},{7,5},{8,10},{9,11},{10,... | collective-permute-start | bytes 3612680 | tf_op jit(solution)/shard_map/ppermute | solution.py:137
  183.2 13.2 %all-to-all-start.3 = ((bf16[2,2,98,768]{3,1,2,0:T(2,128)(2,1)}), bf16[2,2,98,768]{3,1,2,0:T(2,128)(2,1)}, u32[]{:S(2)}, u32[]{:S(2)}) async-start(bf16[2,2,98,768]{3,1,2,0:T(2,128)(2,1)} %copy.123), calls=%async_computation.3 | async-start | bytes 1204224 | tf_op jit(solution)/shard_map/all_to_all | solution.py:175
  196.4 12.5 %all-to-all-start.1 = ((bf16[2,2,98,768]{3,1,2,0:T(2,128)(2,1)}), bf16[2,2,98,768]{3,1,2,0:T(2,128)(2,1)}, u32[]{:S(2)}, u32[]{:S(2)}) async-start(bf16[2,2,98,768]{3,1,2,0:T(2,128)(2,1)} %copy.119), calls=%async_computation.1 | async-start | bytes 1204224 | tf_op jit(solution)/shard_map/all_to_all | solution.py:138
  200.8 62.0 %all-reduce.8.cloned.1.call-start = ((), (), s32[]{:S(2)}) async-start(), calls=%async_computation.11 | async-start | bytes 614400 | tf_op jit(solution)/shard_map/psum | solution.py:240
  222.2 88.6 %reduce-scatter.3.cloned.1.call-start = ((), (), s32[]{:S(2)}) async-start(), calls=%async_computation.12 | async-start | bytes 2949120 | tf_op jit(solution)/shard_map/reduce_scatter | solution.py:183
  225.6 119.7 %reduce-scatter.5.cloned.1.call-start = ((), (), s32[]{:S(2)}) async-start(), calls=%async_computation.13 | async-start | bytes 2949120 | tf_op jit(solution)/shard_map/reduce_scatter | solution.py:186
  233.6 29.2 %copy-start.40 = (f32[768]{0:T(1024)S(1)}, f32[768]{0:T(1024)}, u32[]{:S(2)}) copy-start(f32[768]{0:T(1024)} %param.14) | copy-start | bytes 9220
  233.6 29.2 %copy-start.42 = (f32[197]{0:T(256)S(1)}, f32[197]{0:T(256)}, u32[]{:S(2)}) copy-start(f32[197]{0:T(256)} %copy-done.41) | copy-start | bytes 2368
  233.6 29.2 %copy-start.45 = (f32[768]{0:T(1024)S(1)}, f32[768]{0:T(1024)}, u32[]{:S(2)}) copy-start(f32[768]{0:T(1024)} %param.15) | copy-start | bytes 9220
  235.5 11.9 %all-to-all-start.6 = ((bf16[8,192,96]{2,1,0:T(8,128)(2,1)}), bf16[8,192,96]{2,1,0:T(8,128)(2,1)}, u32[]{:S(2)}, u32[]{:S(2)}) async-start(bf16[8,192,96]{2,1,0:T(8,128)(2,1)} %bitcast.164), calls=%async_computation.6 | async-start | bytes 786432 | tf_op jit(solution)/shard_map/all_to_all | solution.py:21
  249.1 24.5 %copy-start.27 = (bf16[3,64,197]{2,1,0:T(8,128)(2,1)S(1)}, bf16[3,64,197]{2,1,0:T(8,128)(2,1)}, u32[]{:S(2)}) copy-start(bf16[3,64,197]{2,1,0:T(8,128)(2,1)} %copy-done.26) | copy-start | bytes 226948
  268.6 8.3 %all-to-all-start.4 = ((bf16[8,96,8]{1,2,0:T(8,128)(2,1)}), bf16[8,96,8]{1,2,0:T(8,128)(2,1)S(1)}, u32[]{:S(2)}, u32[]{:S(2)}) async-start(bf16[8,96,8]{1,2,0:T(8,128)(2,1)} %concatenate.12), calls=%async_computation.4 | async-start | bytes 32768 | tf_op jit(solution)/shard_map/all_to_all | solution.py:21
  276.9 26.5 %all-to-all-start.5 = ((bf16[8,3,96,192]{3,2,1,0:T(8,128)(2,1)}), bf16[8,3,96,192]{3,2,1,0:T(8,128)(2,1)}, u32[]{:S(2)}, u32[]{:S(2)}) async-start(bf16[8,3,96,192]{3,2,1,0:T(8,128)(2,1)} %copy.137), calls=%async_computation.5 | async-start | bytes 2359296 | tf_op jit(solution)/shard_map/all_to_all | solution.py:21
  (35 other events, 59.8 us)
Sparse Core Ops, SparseCore 0:
  15.4 42.5 all-reduce.3
  120.1 60.7 all-reduce.5
  222.3 40.4 all-reduce.7
  265.2 45.4 reduce-scatter.2
  313.2 32.1 reduce-scatter.4
